TPU v7x, 32 devices: a whole 2x2x4 slice. The times are simulated.
32 devices in a mesh: feat: 8 (over z, y), ex: 4 (over x, core).
Axes of the slice: x: 2, y: 2, z: 4, core: 2. Of those that a mesh axis runs over, the one named last changes fastest.
Arguments:
- examples: bfloat16 [4096, 262144], P('ex', 'feat'), may hold values from -6 to 6
- weights: bfloat16 [262144], P('feat'), may hold values from -0.01171875 to 0.01171875
- labels: int32 [4096], P('ex'), may hold values from 0 to 1
- split: int32 [4096], P('ex'), may hold values 0 or 1
- val_weight: float32 [32, 4096], P(None, 'ex'), may hold values from 0.1 to 10
- strengths: float32 [256], replicated, may hold values from 0.05 to 1
- block_ids: int32 [262144], P('feat'), may hold values from 0 to 255
Outputs:
- solve: float32 [32, 262144], P(None, ('feat', 'ex'))
- hypergrad: float32 [32, 256], P(None, ('feat', 'ex'))
All inputs are finite; a program needn't handle non-finite values. No bound on the sum of `split` on one device may be relied on, other than what follows from the above.
Results may differ from a plain program's by a relative error of at most 0.0029.
Values may be sent and summed in bfloat16 or wider, within the bound.
A program may use at most 128 MiB of HBM per device.

v0:
```python
import jax
import jax.numpy as jnp
from jax import lax
from jax.sharding import PartitionSpec as P


def shards(examples, weights, labels, split, val_weight, strengths, block_ids):
    n_ex = lax.axis_size("ex")
    n_feat = lax.axis_size("feat")
    ex_pos = lax.axis_index("ex")
    feat_pos = lax.axis_index("feat")
    total = examples.shape[0] * n_ex
    width = examples.shape[1]
    share = width // n_ex
    blocks = strengths.shape[0]
    nb_local = blocks // (n_feat * n_ex)
    margin = lax.psum(jnp.dot(examples, weights, preferred_element_type=jnp.float32), "feat")
    prob = 1.0 / (1.0 + jnp.exp(-margin))
    train = split.astype(jnp.float32)
    curvew = train * prob * (1.0 - prob)
    err = (1.0 - train) * (prob - labels.astype(jnp.float32))
    gradw = (val_weight * err[None, :] / jnp.sqrt(jnp.float32(total))).astype(jnp.bfloat16)
    grad_part = jnp.dot(gradw, examples, preferred_element_type=jnp.float32)
    onehot = (block_ids[:, None] == jnp.arange(blocks, dtype=jnp.int32)[None, :]).astype(
        jnp.float32
    )
    lamf = jnp.dot(onehot, strengths, precision=lax.Precision.HIGHEST)
    wfloat = weights.astype(jnp.float32)
    start = ex_pos * share
    rhs = lax.psum_scatter(grad_part, "ex", scatter_dimension=1, tiled=True)
    lam_loc = lax.dynamic_slice_in_dim(lamf, start, share, 0)
    onehot_loc = lax.dynamic_slice_in_dim(onehot, start, share, 0)
    w_loc = lax.dynamic_slice_in_dim(wfloat, start, share, 0)

    def norm_sum(vec):
        return lax.psum(jnp.sum(vec * vec, axis=1), ("feat", "ex"))

    solve = jnp.zeros_like(rhs)
    resid = rhs
    direc = rhs
    norm_now = norm_sum(resid)
    for step in range(2):
        full_dir = lax.all_gather(direc.astype(jnp.bfloat16), "ex", axis=1, tiled=True)
        tang = lax.dot_general(
            full_dir, examples, (((1,), (1,)), ((), ())), preferred_element_type=jnp.float32
        )
        tang = lax.psum(tang, "feat")
        wtang = (curvew[None, :] * tang).astype(jnp.bfloat16)
        prod = lax.psum_scatter(
            jnp.dot(wtang, examples, preferred_element_type=jnp.float32),
            "ex",
            scatter_dimension=1,
            tiled=True,
        )
        image = prod / jnp.float32(total) + lam_loc[None, :] * direc
        alpha = norm_now / lax.psum(jnp.sum(direc * image, axis=1), ("feat", "ex"))
        solve = solve + alpha[:, None] * direc
        resid = resid - alpha[:, None] * image
        if step == 0:
            norm_next = norm_sum(resid)
            direc = resid + (norm_next / norm_now)[:, None] * direc
            norm_now = norm_next
    partial_blocks = jnp.dot(solve * w_loc[None, :], onehot_loc, precision=lax.Precision.HIGHEST)
    block_sums = lax.psum_scatter(partial_blocks, ("feat", "ex"), scatter_dimension=1, tiled=True)
    own = lax.dynamic_slice_in_dim(strengths, (feat_pos * n_ex + ex_pos) * nb_local, nb_local, 0)
    return (solve, -own[None, :] * block_sums)


def solution(mesh):
    placed = (P("ex", "feat"), P("feat"), P("ex"), P("ex"), P(None, "ex"), P(), P("feat"))
    return jax.shard_map(
        shards,
        mesh=mesh,
        in_specs=placed,
        out_specs=(P(None, ("feat", "ex")), P(None, ("feat", "ex"))),
        check_vma=False,
    )
```

profile of v0, /device:TPU:0, one launch (start us, length us, event | category | flops | bytes accessed | tf_op | source)
XLA Modules:
  0.0 695.1 jit_solution(9688805539957404620)
XLA Ops:
  7.2 0.0 reduce-scatter.4.cloned.1.call-start
  7.2 0.9 reshape.14
  8.1 0.0 copy-start.5
  8.1 0.0 copy-start.6
  8.1 0.0 copy-start.3
  8.2 26.6 %fusion.15 = f32[1,1024]{1,0:T(1,128)S(1)} fusion(bf16[1024,32768]{1,0:T(8,128)(2,1)} %param.7, bf16[32768,1]{0,1:T(2,128)(2,1)S(1)} %reshape.14), kind=kOutput, calls=%fused_computation.33 | convolution fusion | flops 67108864 | bytes 67178496 | tf_op jit(solution)/shard_map/dot_general | solution.py:17
  34.8 23.2 %psum.49 = f32[1024]{0:T(1024)S(1)} all-reduce(f32[1024]{0:T(1024)S(1)} %bitcast.13), channel_id=1, replica_groups=mesh['feat'=8,'ex'=4] {'feat'}, use_global_device_ids=true, to_apply=%region_0.0 | all-reduce | flops 1024 | bytes 8192 | tf_op jit(solution)/shard_map/psum | solution.py:17
  58.0 0.0 copy-done.5
  58.0 0.0 copy-done.6
  58.0 0.0 copy-done.3
  58.0 25.3 %fusion.5 = f32[32,32768]{1,0:T(8,128)} fusion(bf16[1024,32768]{1,0:T(8,128)(2,1)} %param.7, f32[32,1024]{1,0:T(8,128)S(1)} %copy-done.3, f32[1024]{0:T(1024)S(1)} %get-tuple-element.7), kind=kOutput, calls=%fused_computation.17 | convolution fusion | flops 2147581952 | bytes 71438336 | tf_op jit(solution)/shard_map/dot_general | solution.py:23
  83.3 0.0 reduce-scatter.4.cloned.1.call-update
  83.3 0.0 all-gather.3.cloned.1.call-start
  83.3 41.8 %reduce-scatter.4.cloned.1.call-done = f32[32,8192]{1,0:T(8,128)} async-done(((f32[32,32768]{1,0:T(8,128)}), f32[32,8192]{1,0:T(8,128)}) %reduce-scatter.4.cloned.1.call-update) | async-done | bytes 1048592 | tf_op jit(solution)/shard_map/reduce_scatter | solution.py:30
  125.2 2.1 convert_element_type.28
  127.2 0.0 all-gather.3.cloned.1.call-update
  127.2 0.0 all-reduce.5.cloned.1.call-start
  127.3 22.7 %all-gather.3.cloned.1.call-done = bf16[32,32768]{1,0:T(8,128)(2,1)} async-done(((bf16[32,8192]{1,0:T(8,128)(2,1)}), bf16[32,32768]{1,0:T(8,128)(2,1)}) %all-gather.3.cloned.1.call-update) | async-done | bytes 2097168 | tf_op jit(solution)/shard_map/all_gather | solution.py:43
  150.0 27.6 %fusion.16 = f32[32,1024]{1,0:T(8,128)} fusion(bf16[32,32768]{1,0:T(8,128)(2,1)} %all-gather.3.cloned.1.call-done, bf16[1024,32768]{1,0:T(8,128)(2,1)} %param.7), kind=kOutput, calls=%fused_computation.34 | convolution fusion | flops 2147483648 | bytes 69337088 | tf_op jit(solution)/shard_map/dot_general | solution.py:44
  177.6 0.0 all-reduce.5.cloned.1.call-update
  177.6 0.0 reduce-scatter.6.cloned.1.call-start
  177.7 70.5 %all-reduce.5.cloned.1.call-done = f32[32,1024]{1,0:T(8,128)} async-done(((f32[32,1024]{1,0:T(8,128)}), f32[32,1024]{1,0:T(8,128)}) %all-reduce.5.cloned.1.call-update) | async-done | bytes 131088 | tf_op jit(solution)/shard_map/psum | solution.py:47
  248.2 0.0 copy-start.4
  248.2 0.0 copy-start.7
  248.2 26.5 %fusion.6 = f32[32,32768]{1,0:T(8,128)} fusion(bf16[1024,32768]{1,0:T(8,128)(2,1)} %param.7, f32[32,1024]{1,0:T(8,128)} %all-reduce.5.cloned.1.call-done, f32[1024]{0:T(1024)S(1)} %get-tuple-element.6), kind=kOutput, calls=%fused_computation.18 | convolution fusion | flops 2147549184 | bytes 71438336 | tf_op jit(solution)/shard_map/dot_general | solution.py:50
  274.6 0.0 copy-start
  274.6 0.0 reduce-scatter.6.cloned.1.call-update
  274.7 0.0 all-gather.5.cloned.1.call-start
  274.7 0.0 copy-done.4
  274.7 0.0 copy-done.7
  274.7 17.1 %fusion.3 = f32[1,32768]{1,0:T(1,128)S(1)} fusion(f32[256,1]{0,1:T(1,128)S(1)} %bitcast.15, s32[32768]{0:T(1024)S(1)} %copy-done.4), kind=kOutput, calls=%fused_computation.12 | convolution fusion | flops 109051904 | bytes 263168 | tf_op jit(solution)/shard_map/dot_general | solution.py:27
  291.8 26.6 %reduce-scatter.6.cloned.1.call-done = f32[32,8192]{1,0:T(8,128)} async-done(((f32[32,32768]{1,0:T(8,128)}), f32[32,8192]{1,0:T(8,128)}) %reduce-scatter.6.cloned.1.call-update) | async-done | bytes 1048592 | tf_op jit(solution)/shard_map/reduce_scatter | solution.py:49
  318.4 0.0 copy-done
  318.4 1.6 multiply_reduce_fusion.2
  320.0 39.3 %all-reduce.1 = (f32[32]{0:T(128)S(1)}, f32[32]{0:T(128)S(1)}) all-reduce(f32[32]{0:T(128)S(1)} %get-tuple-element.3, f32[32]{0:T(128)S(1)} %get-tuple-element.2), channel_id=1, replica_groups=mesh['feat'=8,'ex'=4] {'feat','ex'}, use_global_device_ids=true, to_apply=%region_3.0 | all-reduce | flops 64 | bytes 512 | tf_op jit(solution)/shard_map/psum | solution.py:36
  359.3 1.6 multiply_reduce_fusion.1
  360.9 41.1 %psum.53 = f32[32]{0:T(128)S(1)} all-reduce(f32[32]{0:T(128)S(1)} %multiply_reduce_fusion.1), channel_id=1, replica_groups=mesh['feat'=8,'ex'=4] {'feat','ex'}, use_global_device_ids=true, to_apply=%region_9.0 | all-reduce | flops 32 | bytes 256 | tf_op jit(solution)/shard_map/psum | solution.py:36
  402.0 2.3 fusion.14
  404.3 0.0 all-gather.5.cloned.1.call-update
  404.3 0.0 all-reduce.7.cloned.1.call-start
  404.4 22.5 %all-gather.5.cloned.1.call-done = bf16[32,32768]{1,0:T(8,128)(2,1)} async-done(((bf16[32,8192]{1,0:T(8,128)(2,1)}), bf16[32,32768]{1,0:T(8,128)(2,1)}) %all-gather.5.cloned.1.call-update) | async-done | bytes 2097168 | tf_op jit(solution)/shard_map/all_gather | solution.py:43
  426.8 27.6 %fusion.17 = f32[32,1024]{1,0:T(8,128)} fusion(bf16[32,32768]{1,0:T(8,128)(2,1)} %all-gather.5.cloned.1.call-done, bf16[1024,32768]{1,0:T(8,128)(2,1)} %param.7), kind=kOutput, calls=%fused_computation.35 | convolution fusion | flops 2147483648 | bytes 69337088 | tf_op jit(solution)/shard_map/dot_general | solution.py:44
  454.5 0.0 all-reduce.7.cloned.1.call-update
  454.5 0.0 reduce-scatter.8.cloned.1.call-start
  454.5 70.5 %all-reduce.7.cloned.1.call-done = f32[32,1024]{1,0:T(8,128)} async-done(((f32[32,1024]{1,0:T(8,128)}), f32[32,1024]{1,0:T(8,128)}) %all-reduce.7.cloned.1.call-update) | async-done | bytes 131088 | tf_op jit(solution)/shard_map/psum | solution.py:47
  525.0 26.4 %fusion.7 = f32[32,32768]{1,0:T(8,128)} fusion(bf16[1024,32768]{1,0:T(8,128)(2,1)} %param.7, f32[32,1024]{1,0:T(8,128)} %all-reduce.7.cloned.1.call-done, f32[1024]{0:T(1024)S(1)} %get-tuple-element.6), kind=kOutput, calls=%fused_computation.19 | convolution fusion | flops 2147549184 | bytes 71438336 | tf_op jit(solution)/shard_map/dot_general | solution.py:50
  551.5 0.0 copy-start.1
  551.5 0.0 reduce-scatter.8.cloned.1.call-update
  551.5 0.1 dynamic-slice_negate_fusion
  551.6 0.8 dynamic-slice_convert_fusion
  552.4 15.8 %iota_compare_fusion = pred[32768,256]{1,0:T(32,128)(4,1)} fusion(s32[32768]{0:T(1024)S(1)} %copy-done.4), kind=kLoop, calls=%fused_computation | loop fusion | flops 8388608 | bytes 8519680 | tf_op jit(solution)/shard_map/eq | solution.py:24
  568.2 27.0 %reduce-scatter.8.cloned.1.call-done = f32[32,8192]{1,0:T(8,128)} async-done(((f32[32,32768]{1,0:T(8,128)}), f32[32,8192]{1,0:T(8,128)}) %reduce-scatter.8.cloned.1.call-update) | async-done | bytes 1048592 | tf_op jit(solution)/shard_map/reduce_scatter | solution.py:49
  595.2 0.0 copy-done.1
  595.2 1.8 multiply_reduce_fusion
  597.0 39.5 %psum.55 = f32[32]{0:T(128)S(1)} all-reduce(f32[32]{0:T(128)S(1)} %multiply_reduce_fusion), channel_id=1, replica_groups=mesh['feat'=8,'ex'=4] {'feat','ex'}, use_global_device_ids=true, to_apply=%region_13.0 | all-reduce | flops 32 | bytes 256 | tf_op jit(solution)/shard_map/psum | solution.py:56
  636.5 0.4 multiply_add_fusion
  636.9 0.0 copy-start.2
  637.0 8.6 %fusion = f32[32,256]{0,1:T(8,128)S(1)} fusion(pred[32768,256]{1,0:T(32,128)(4,1)} %iota_compare_fusion, s32[]{:T(128)S(6)} %select_n.8, f32[32,8192]{1,0:T(8,128)S(1)} %multiply_add_fusion, f32[8192]{0:T(1024)S(1)} %dynamic-slice_convert_fusion), kind=kOutput, calls=%fused_computation.1 | convolution fusion | flops 805568512 | bytes 3211268 | tf_op jit(solution)/shard_map/dot_general | solution.py:63
  645.6 42.0 %all-reduce = f32[32,256]{0,1:T(8,128)S(1)} all-reduce(f32[32,256]{0,1:T(8,128)S(1)} %fusion), channel_id=5, replica_groups=mesh['feat'=8,'ex'=4] {'feat','ex'}, use_global_device_ids=true, to_apply=%region_14.0.clone | all-reduce | flops 8192 | bytes 65536
  687.6 0.7 dynamic-slice_multiply_fusion
  688.3 0.0 copy-done.2
  (5 shorter events, 0.0 us)
Async XLA Ops:
  7.2 118.0 %reduce-scatter.4.cloned.1.call-start = ((), (), s32[]{:S(2)}) async-start(), calls=%async_computation.3 | async-start | bytes 5242880 | tf_op jit(solution)/shard_map/reduce_scatter | solution.py:30
  8.1 49.8 %copy-start.5 = (s32[1024]{0:T(1024)S(1)}, s32[1024]{0:T(1024)}, u32[]{:S(2)}) copy-start(s32[1024]{0:T(1024)} %param.10) | copy-start | bytes 12292
  8.1 49.8 %copy-start.6 = (s32[1024]{0:T(1024)S(1)}, s32[1024]{0:T(1024)}, u32[]{:S(2)}) copy-start(s32[1024]{0:T(1024)} %param.9) | copy-start | bytes 12292
  8.1 49.8 %copy-start.3 = (f32[32,1024]{1,0:T(8,128)S(1)}, f32[32,1024]{1,0:T(8,128)}, u32[]{:S(2)}) copy-start(f32[32,1024]{1,0:T(8,128)} %param.11) | copy-start | bytes 393220
  83.3 66.7 %all-gather.3.cloned.1.call-start = ((), (), s32[]{:S(2)}) async-start(), calls=%async_computation.4 | async-start | bytes 2621440 | tf_op jit(solution)/shard_map/all_gather | solution.py:43
  127.2 120.9 %all-reduce.5.cloned.1.call-start = ((), (), s32[]{:S(2)}) async-start(), calls=%async_computation.5 | async-start | bytes 262144 | tf_op jit(solution)/shard_map/psum | solution.py:47
  177.6 140.8 %reduce-scatter.6.cloned.1.call-start = ((), (), s32[]{:S(2)}) async-start(), calls=%async_computation.6 | async-start | bytes 5242880 | tf_op jit(solution)/shard_map/reduce_scatter | solution.py:49
  248.2 26.5 %copy-start.4 = (s32[32768]{0:T(1024)S(1)}, s32[32768]{0:T(1024)}, u32[]{:S(2)}) copy-start(s32[32768]{0:T(1024)} %param.13) | copy-start | bytes 393220
  248.2 26.6 %copy-start.7 = (f32[256]{0:T(256)S(1)}, f32[256]{0:T(256)}, u32[]{:S(2)}) copy-start(f32[256]{0:T(256)} %param.12) | copy-start | bytes 3076
  274.6 43.8 %copy-start = (f32[32,8192]{1,0:T(8,128)S(1)}, f32[32,8192]{1,0:T(8,128)}, u32[]{:S(2)}) copy-start(f32[32,8192]{1,0:T(8,128)} %reduce-scatter.4.cloned.1.call-done) | copy-start | bytes 3145732
  274.7 152.2 %all-gather.5.cloned.1.call-start = ((), (), s32[]{:S(2)}) async-start(), calls=%async_computation.7 | async-start | bytes 2621440 | tf_op jit(solution)/shard_map/all_gather | solution.py:43
  404.3 120.7 %all-reduce.7.cloned.1.call-start = ((), (), s32[]{:S(2)}) async-start(), calls=%async_computation.8 | async-start | bytes 262144 | tf_op jit(solution)/shard_map/psum | solution.py:47
  454.5 140.7 %reduce-scatter.8.cloned.1.call-start = ((), (), s32[]{:S(2)}) async-start(), calls=%async_computation.9 | async-start | bytes 5242880 | tf_op jit(solution)/shard_map/reduce_scatter | solution.py:49
  551.5 43.7 %copy-start.1 = (f32[32,8192]{1,0:T(8,128)S(1)}, f32[32,8192]{1,0:T(8,128)}, u32[]{:S(2)}) copy-start(f32[32,8192]{1,0:T(8,128)} %reduce-scatter.6.cloned.1.call-done) | copy-start | bytes 3145732
  636.9 51.3 %copy-start.2 = (f32[32,8192]{1,0:T(8,128)}, f32[32,8192]{1,0:T(8,128)S(1)}, u32[]{:S(2)}) copy-start(f32[32,8192]{1,0:T(8,128)S(1)} %multiply_add_fusion) | copy-start | bytes 3145732
Sparse Core Ops, SparseCore 0:
  83.4 41.7 reduce-scatter.3
  127.4 22.5 all-gather.2
  177.7 70.3 all-reduce.4
  274.8 43.5 reduce-scatter.5
  404.4 22.3 all-gather.4
  454.6 70.3 all-reduce.6
  551.6 43.5 reduce-scatter.7
where the time goes:
time: 696 us; the launch traced here: 695 us
  waiting for transfers between devices  282 us (41%)
  matrix products  186 us (27%)
  blocking collectives  185 us (27%)
  other arithmetic  27.1 us (4%)
  between operations  14.3 us (2%)
    psum x2, waiting for transfers between devices, shards(): tang = lax.psum(tang, 'feat')  141 us
    psum x2, blocking collectives, norm_sum(): return lax.psum(jnp.sum(vec * vec, axis=1), ('feat', 'ex'))  80.4 us
    dot_general x2, matrix products, shards(): lax.dot_general(full_dir, examples, (((1,), (1,)), ((), ())), preferred_e...  55.3 us
    reduce_scatter x2, waiting for transfers between devices, shards(): lax.psum_scatter(jnp.dot(wtang, examples, preferred_element_type=jnp.floa...  53.6 us
    dot_general x2, matrix products, shards(): jnp.dot(wtang, examples, preferred_element_type=jnp.float32)  52.9 us
    all_gather x2, waiting for transfers between devices, shards(): lax.all_gather(direc.astype(jnp.bfloat16), 'ex', axis=1, tiled=True)  45.1 us
    unnamed x1, blocking collectives  42 us
    reduce_scatter x1, waiting for transfers between devices, shards(): rhs = lax.psum_scatter(grad_part, 'ex', scatter_dimension=1, tiled=True)  41.8 us
  transfers between devices with their start and end apart: 7, of which 7 were waited for; matrix products, arithmetic and copies ran while one was open for 5% of the time, Pallas kernels for 0%

commit v1 on v0

--- a/solution.py
+++ b/solution.py
@@ -2,6 +2,24 @@
 import jax.numpy as jnp
 from jax import lax
 from jax.sharding import PartitionSpec as P
+
+
+def gather_around(value, axis, dim):
+    ways, here, step = (lax.axis_size(axis), lax.axis_index(axis), value.shape[dim])
+    shape = [n * ways if d == dim else n for d, n in enumerate(value.shape)]
+    full = lax.dynamic_update_slice_in_dim(
+        jnp.zeros(shape, value.dtype), value, here * step, axis=dim
+    )
+    going_up = going_down = value
+    for far in range(1, ways // 2 + 1):
+        going_up = lax.ppermute(going_up, axis, [(d, (d + 1) % ways) for d in range(ways)])
+        full = lax.dynamic_update_slice_in_dim(full, going_up, (here - far) % ways * step, axis=dim)
+        if 2 * far < ways:
+            going_down = lax.ppermute(going_down, axis, [(d, (d - 1) % ways) for d in range(ways)])
+            full = lax.dynamic_update_slice_in_dim(
+                full, going_down, (here + far) % ways * step, axis=dim
+            )
+    return full
 
 
 def shards(examples, weights, labels, split, val_weight, strengths, block_ids):
@@ -40,7 +58,7 @@
     direc = rhs
     norm_now = norm_sum(resid)
     for step in range(2):
-        full_dir = lax.all_gather(direc.astype(jnp.bfloat16), "ex", axis=1, tiled=True)
+        full_dir = gather_around(direc.astype(jnp.bfloat16), "ex", 1)
         tang = lax.dot_general(
             full_dir, examples, (((1,), (1,)), ((), ())), preferred_element_type=jnp.float32
         )

time: 696 us -> 695 us (level)
  waiting for transfers between devices: 282 us -> 273 us
    all_gather x2 -> x0, waiting for transfers between devices: 45.1 us -> none  [shards(): lax.all_gather(direc.astype(jnp.bfloat16), 'ex', axis=1, tiled=True)]
    ppermute x0 -> x6, waiting for transfers between devices: none -> 34.8 us  [the longest x4 34.8 us: gather_around(): lax.ppermute(going_up, axis, [(d, (d + 1) % ways) for d in range(ways)])]
  transfers between devices with their start and end apart: 7 -> 11, of which waited for: 7 -> 9; matrix products, arithmetic and copies ran while one was open for 5% -> 5% of each run, Pallas kernels for 0% -> 0%
where the time goes in v1:
time: 695 us; the launch traced here: 694 us
  waiting for transfers between devices  273 us (39%)
  matrix products  185 us (27%)
  blocking collectives  185 us (27%)
  other arithmetic  25.2 us (4%)
  between operations  14 us (2%)
    psum x2, waiting for transfers between devices, shards(): tang = lax.psum(tang, 'feat')  143 us
    psum x2, blocking collectives, norm_sum(): return lax.psum(jnp.sum(vec * vec, axis=1), ('feat', 'ex'))  80.5 us
    dot_general x2, matrix products, shards(): lax.dot_general(full_dir, examples, (((1,), (1,)), ((), ())), preferred_e...  54.8 us
    reduce_scatter x2, waiting for transfers between devices, shards(): lax.psum_scatter(jnp.dot(wtang, examples, preferred_element_type=jnp.floa...  52.9 us
    dot_general x2, matrix products, shards(): jnp.dot(wtang, examples, preferred_element_type=jnp.float32)  52.8 us
    unnamed x1, blocking collectives  42 us
    reduce_scatter x1, waiting for transfers between devices, shards(): rhs = lax.psum_scatter(grad_part, 'ex', scatter_dimension=1, tiled=True)  41.8 us
    psum x1, blocking collectives, shards(): alpha = norm_now / lax.psum(jnp.sum(direc * image, axis=1), ('feat', 'ex'))  39.6 us
  transfers between devices with their start and end apart: 11, of which 9 were waited for; matrix products, arithmetic and copies ran while one was open for 5% of the time, Pallas kernels for 0%

profile of v1, /device:TPU:0, one launch (start us, length us, event | category | flops | bytes accessed | tf_op | source)
XLA Modules:
  0.0 694.3 jit_solution(10393611718604456008)
XLA Ops:
  7.2 0.0 reduce-scatter.4.cloned.1.call-start
  7.2 0.9 reshape.14
  8.1 0.0 copy-start.5
  8.1 0.0 copy-start.6
  8.1 0.0 copy-start.3
  8.2 26.6 %fusion.16 = f32[1,1024]{1,0:T(1,128)S(1)} fusion(bf16[1024,32768]{1,0:T(8,128)(2,1)} %param.7, bf16[32768,1]{0,1:T(2,128)(2,1)S(1)} %reshape.14), kind=kOutput, calls=%fused_computation.41 | convolution fusion | flops 67108864 | bytes 67178496 | tf_op jit(solution)/shard_map/dot_general | solution.py:35
  34.8 23.2 %psum.49 = f32[1024]{0:T(1024)S(1)} all-reduce(f32[1024]{0:T(1024)S(1)} %bitcast.13), channel_id=1, replica_groups=mesh['feat'=8,'ex'=4] {'feat'}, use_global_device_ids=true, to_apply=%region_0.0 | all-reduce | flops 1024 | bytes 8192 | tf_op jit(solution)/shard_map/psum | solution.py:35
  58.0 0.0 copy-done.5
  58.0 0.0 copy-done.6
  58.0 25.3 %fusion.5 = f32[32,32768]{1,0:T(8,128)} fusion(bf16[1024,32768]{1,0:T(8,128)(2,1)} %param.7, f32[32,1024]{1,0:T(8,128)S(1)} %copy-done.3, f32[1024]{0:T(1024)S(1)} %get-tuple-element.11), kind=kOutput, calls=%fused_computation.17 | convolution fusion | flops 2147581952 | bytes 71438336 | tf_op jit(solution)/shard_map/dot_general | solution.py:41
  83.3 0.0 reduce-scatter.4.cloned.1.call-update
  83.3 0.0 all-reduce.5.cloned.1.call-start
  83.3 41.8 %reduce-scatter.4.cloned.1.call-done = f32[32,8192]{1,0:T(8,128)} async-done(((f32[32,32768]{1,0:T(8,128)}), f32[32,8192]{1,0:T(8,128)}) %reduce-scatter.4.cloned.1.call-update) | async-done | bytes 1048592 | tf_op jit(solution)/shard_map/reduce_scatter | solution.py:48
  125.2 0.1 broadcast.25.clone
  125.3 1.3 constant_dynamic-update-slice_fusion.7
  126.6 0.1 collective-permute-start
  126.7 1.7 collective-permute-start.1
  128.4 11.8 %collective-permute-done = bf16[32,8192]{1,0:T(8,128)(2,1)S(1)} collective-permute-done((bf16[32,8192]{1,0:T(8,128)(2,1)S(1)}, bf16[32,8192]{1,0:T(8,128)(2,1)S(1)}, u32[]{:S(2)}, u32[]{:S(2)}) %collective-permute-start) | collective-permute-done | bytes 524320 | tf_op jit(solution)/shard_map/ppermute | solution.py:15
  140.2 0.0 collective-permute-start.2
  140.3 0.0 collective-permute-done.1
  140.3 8.5 %collective-permute-done.2 = bf16[32,8192]{1,0:T(8,128)(2,1)S(1)} collective-permute-done((bf16[32,8192]{1,0:T(8,128)(2,1)S(1)}, bf16[32,8192]{1,0:T(8,128)(2,1)S(1)}, u32[]{:S(2)}, u32[]{:S(2)}) %collective-permute-start.2) | collective-permute-done | bytes 524320 | tf_op jit(solution)/shard_map/ppermute | solution.py:15
  148.9 27.2 %fusion.17 = f32[32,1024]{1,0:T(8,128)} fusion(bf16[32,32768]{1,0:T(8,128)(2,1)S(1)} %constant_dynamic-update-slice_fusion.4, bf16[1024,32768]{1,0:T(8,128)(2,1)} %param.7), kind=kOutput, calls=%fused_computation.42 | convolution fusion | flops 2147483648 | bytes 69337088 | tf_op jit(solution)/shard_map/dot_general | solution.py:62
  176.1 0.0 all-reduce.5.cloned.1.call-update
  176.1 0.0 reduce-scatter.6.cloned.1.call-start
  176.1 70.3 %all-reduce.5.cloned.1.call-done = f32[32,1024]{1,0:T(8,128)} async-done(((f32[32,1024]{1,0:T(8,128)}), f32[32,1024]{1,0:T(8,128)}) %all-reduce.5.cloned.1.call-update) | async-done | bytes 131088 | tf_op jit(solution)/shard_map/psum | solution.py:65
  246.4 26.4 %fusion.6 = f32[32,32768]{1,0:T(8,128)} fusion(bf16[1024,32768]{1,0:T(8,128)(2,1)} %param.7, f32[32,1024]{1,0:T(8,128)} %all-reduce.5.cloned.1.call-done, f32[1024]{0:T(1024)S(1)} %get-tuple-element.10), kind=kOutput, calls=%fused_computation.18 | convolution fusion | flops 2147549184 | bytes 71438336 | tf_op jit(solution)/shard_map/dot_general | solution.py:68
  272.9 0.0 reduce-scatter.6.cloned.1.call-update
  272.9 0.0 all-reduce.7.cloned.1.call-start
  272.9 0.8 copy-done.4
  273.8 17.0 %fusion.3 = f32[1,32768]{1,0:T(1,128)S(1)} fusion(f32[256,1]{0,1:T(1,128)S(1)} %bitcast.15, s32[32768]{0:T(1024)S(1)} %copy-done.4), kind=kOutput, calls=%fused_computation.12 | convolution fusion | flops 109051904 | bytes 263168 | tf_op jit(solution)/shard_map/dot_general | solution.py:45
  290.8 25.8 %reduce-scatter.6.cloned.1.call-done = f32[32,8192]{1,0:T(8,128)} async-done(((f32[32,32768]{1,0:T(8,128)}), f32[32,8192]{1,0:T(8,128)}) %reduce-scatter.6.cloned.1.call-update) | async-done | bytes 1048592 | tf_op jit(solution)/shard_map/reduce_scatter | solution.py:67
  316.6 0.0 copy-done
  316.6 1.7 multiply_reduce_fusion.2
  318.3 39.5 %all-reduce.1 = (f32[32]{0:T(128)S(1)}, f32[32]{0:T(128)S(1)}) all-reduce(f32[32]{0:T(128)S(1)} %get-tuple-element.3, f32[32]{0:T(128)S(1)} %get-tuple-element.2), channel_id=1, replica_groups=mesh['feat'=8,'ex'=4] {'feat','ex'}, use_global_device_ids=true, to_apply=%region_3.0 | all-reduce | flops 64 | bytes 512 | tf_op jit(solution)/shard_map/psum | solution.py:54
  357.8 1.6 multiply_reduce_fusion.1
  359.4 41.0 %psum.53 = f32[32]{0:T(128)S(1)} all-reduce(f32[32]{0:T(128)S(1)} %multiply_reduce_fusion.1), channel_id=1, replica_groups=mesh['feat'=8,'ex'=4] {'feat','ex'}, use_global_device_ids=true, to_apply=%region_9.10 | all-reduce | flops 32 | bytes 256 | tf_op jit(solution)/shard_map/psum | solution.py:54
  400.4 1.5 broadcast.25
  401.9 1.1 constant_dynamic-update-slice_fusion.3
  403.0 0.0 collective-permute-start.3
  403.0 1.7 collective-permute-start.4
  404.7 9.9 %collective-permute-done.3 = bf16[32,8192]{1,0:T(8,128)(2,1)S(1)} collective-permute-done((bf16[32,8192]{1,0:T(8,128)(2,1)S(1)}, bf16[32,8192]{1,0:T(8,128)(2,1)S(1)}, u32[]{:S(2)}, u32[]{:S(2)}) %collective-permute-start.3) | collective-permute-done | bytes 524320 | tf_op jit(solution)/shard_map/ppermute | solution.py:15
  414.6 2.4 collective-permute-start.5
  417.0 0.9 constant_dynamic-update-slice_fusion.2
  417.9 0.0 collective-permute-done.4
  417.9 0.8 constant_dynamic-update-slice_fusion.1
  418.7 4.6 collective-permute-done.5
  423.3 0.8 constant_dynamic-update-slice_fusion
  424.1 27.6 %fusion.18 = f32[32,1024]{1,0:T(8,128)} fusion(bf16[32,32768]{1,0:T(8,128)(2,1)} %constant_dynamic-update-slice_fusion, bf16[1024,32768]{1,0:T(8,128)(2,1)} %param.7), kind=kOutput, calls=%fused_computation.43 | convolution fusion | flops 2147483648 | bytes 69337088 | tf_op jit(solution)/shard_map/dot_general | solution.py:62
  451.7 0.0 all-reduce.7.cloned.1.call-update
  451.7 0.0 reduce-scatter.8.cloned.1.call-start
  451.8 72.7 %all-reduce.7.cloned.1.call-done = f32[32,1024]{1,0:T(8,128)} async-done(((f32[32,1024]{1,0:T(8,128)}), f32[32,1024]{1,0:T(8,128)}) %all-reduce.7.cloned.1.call-update) | async-done | bytes 131088 | tf_op jit(solution)/shard_map/psum | solution.py:65
  524.5 26.4 %fusion.7 = f32[32,32768]{1,0:T(8,128)} fusion(bf16[1024,32768]{1,0:T(8,128)(2,1)} %param.7, f32[32,1024]{1,0:T(8,128)} %all-reduce.7.cloned.1.call-done, f32[1024]{0:T(1024)S(1)} %get-tuple-element.10), kind=kOutput, calls=%fused_computation.19 | convolution fusion | flops 2147549184 | bytes 71438336 | tf_op jit(solution)/shard_map/dot_general | solution.py:68
  550.9 0.0 reduce-scatter.8.cloned.1.call-update
  550.9 0.1 dynamic-slice_negate_fusion
  551.0 0.7 dynamic-slice_convert_fusion
  551.7 15.8 %iota_compare_fusion = pred[32768,256]{1,0:T(32,128)(4,1)} fusion(s32[32768]{0:T(1024)S(1)} %copy-done.4), kind=kLoop, calls=%fused_computation | loop fusion | flops 8388608 | bytes 8519680 | tf_op jit(solution)/shard_map/eq | solution.py:42
  567.6 27.1 %reduce-scatter.8.cloned.1.call-done = f32[32,8192]{1,0:T(8,128)} async-done(((f32[32,32768]{1,0:T(8,128)}), f32[32,8192]{1,0:T(8,128)}) %reduce-scatter.8.cloned.1.call-update) | async-done | bytes 1048592 | tf_op jit(solution)/shard_map/reduce_scatter | solution.py:67
  594.7 1.8 multiply_reduce_fusion
  596.5 39.6 %psum.55 = f32[32]{0:T(128)S(1)} all-reduce(f32[32]{0:T(128)S(1)} %multiply_reduce_fusion), channel_id=1, replica_groups=mesh['feat'=8,'ex'=4] {'feat','ex'}, use_global_device_ids=true, to_apply=%region_13.14 | all-reduce | flops 32 | bytes 256 | tf_op jit(solution)/shard_map/psum | solution.py:74
  636.0 0.4 multiply_add_fusion
  636.4 0.0 copy-start.2
  636.4 8.6 %fusion = f32[32,256]{0,1:T(8,128)S(1)} fusion(pred[32768,256]{1,0:T(32,128)(4,1)} %iota_compare_fusion, s32[]{:T(128)S(6)} %select_n.43, f32[32,8192]{1,0:T(8,128)S(1)} %multiply_add_fusion, f32[8192]{0:T(1024)S(1)} %dynamic-slice_convert_fusion), kind=kOutput, calls=%fused_computation.1 | convolution fusion | flops 805568512 | bytes 3211268 | tf_op jit(solution)/shard_map/dot_general | solution.py:81
  645.1 42.0 %all-reduce = f32[32,256]{0,1:T(8,128)S(1)} all-reduce(f32[32,256]{0,1:T(8,128)S(1)} %fusion), channel_id=5, replica_groups=mesh['feat'=8,'ex'=4] {'feat','ex'}, use_global_device_ids=true, to_apply=%region_14.15.clone | all-reduce | flops 8192 | bytes 65536
  687.1 0.7 dynamic-slice_multiply_fusion
  (16 shorter events, 0.2 us)
Async XLA Ops:
  7.2 118.0 %reduce-scatter.4.cloned.1.call-start = ((), (), s32[]{:S(2)}) async-start(), calls=%async_computation.3 | async-start | bytes 5242880 | tf_op jit(solution)/shard_map/reduce_scatter | solution.py:48
  8.1 49.8 %copy-start.5 = (s32[1024]{0:T(1024)S(1)}, s32[1024]{0:T(1024)}, u32[]{:S(2)}) copy-start(s32[1024]{0:T(1024)} %param.10) | copy-start | bytes 12292
  8.1 49.8 %copy-start.6 = (s32[1024]{0:T(1024)S(1)}, s32[1024]{0:T(1024)}, u32[]{:S(2)}) copy-start(s32[1024]{0:T(1024)} %param.9) | copy-start | bytes 12292
  8.1 49.8 %copy-start.3 = (f32[32,1024]{1,0:T(8,128)S(1)}, f32[32,1024]{1,0:T(8,128)}, u32[]{:S(2)}) copy-start(f32[32,1024]{1,0:T(8,128)} %param.11) | copy-start | bytes 393220
  83.3 163.2 %all-reduce.5.cloned.1.call-start = ((), (), s32[]{:S(2)}) async-start(), calls=%async_computation.4 | async-start | bytes 262144 | tf_op jit(solution)/shard_map/psum | solution.py:65
  126.6 13.6 %collective-permute-start = (bf16[32,8192]{1,0:T(8,128)(2,1)S(1)}, bf16[32,8192]{1,0:T(8,128)(2,1)S(1)}, u32[]{:S(2)}, u32[]{:S(2)}) collective-permute-start(bf16[32,8192]{1,0:T(8,128)(2,1)S(1)} %get-tuple-element.9), channel_id=1, source_target_pairs={{0,1},{1,2},{2,3},{3,0},{4,5},{5,6},{6,7},{7,4},{8,9},{9,10},{10,1... | collective-permute-start | bytes 1572872 | tf_op jit(solution)/shard_map/ppermute | solution.py:15
  126.7 13.5 %collective-permute-start.1 = (bf16[32,8192]{1,0:T(8,128)(2,1)S(1)}, bf16[32,8192]{1,0:T(8,128)(2,1)S(1)}, u32[]{:S(2)}, u32[]{:S(2)}) collective-permute-start(bf16[32,8192]{1,0:T(8,128)(2,1)S(1)} %get-tuple-element.9), channel_id=1, source_target_pairs={{0,3},{1,0},{2,1},{3,2},{4,7},{5,4},{6,5},{7,6},{8,11},{9,8},{10,9... | collective-permute-start | bytes 1572872 | tf_op jit(solution)/shard_map/ppermute | solution.py:18
  140.2 8.6 %collective-permute-start.2 = (bf16[32,8192]{1,0:T(8,128)(2,1)S(1)}, bf16[32,8192]{1,0:T(8,128)(2,1)S(1)}, u32[]{:S(2)}, u32[]{:S(2)}) collective-permute-start(bf16[32,8192]{1,0:T(8,128)(2,1)S(1)} %collective-permute-done), channel_id=1, source_target_pairs={{0,1},{1,2},{2,3},{3,0},{4,5},{5,6},{6,7},{7,4},{8,9},{9,10},{10,1... | collective-permute-start | bytes 1572872 | tf_op jit(solution)/shard_map/ppermute | solution.py:15
  176.1 140.5 %reduce-scatter.6.cloned.1.call-start = ((), (), s32[]{:S(2)}) async-start(), calls=%async_computation.5 | async-start | bytes 5242880 | tf_op jit(solution)/shard_map/reduce_scatter | solution.py:67
  272.9 0.9 copy-start.4
  272.9 0.9 copy-start.7
  272.9 251.6 %all-reduce.7.cloned.1.call-start = ((), (), s32[]{:S(2)}) async-start(), calls=%async_computation.6 | async-start | bytes 262144 | tf_op jit(solution)/shard_map/psum | solution.py:65
  273.8 42.8 %copy-start = (f32[32,8192]{1,0:T(8,128)S(1)}, f32[32,8192]{1,0:T(8,128)}, u32[]{:S(2)}) copy-start(f32[32,8192]{1,0:T(8,128)} %reduce-scatter.4.cloned.1.call-done) | copy-start | bytes 3145732
  316.6 85.3 %copy-start.1 = (f32[32,8192]{1,0:T(8,128)S(1)}, f32[32,8192]{1,0:T(8,128)}, u32[]{:S(2)}) copy-start(f32[32,8192]{1,0:T(8,128)} %reduce-scatter.6.cloned.1.call-done) | copy-start | bytes 3145732
  403.0 11.7 %collective-permute-start.3 = (bf16[32,8192]{1,0:T(8,128)(2,1)S(1)}, bf16[32,8192]{1,0:T(8,128)(2,1)S(1)}, u32[]{:S(2)}, u32[]{:S(2)}) collective-permute-start(bf16[32,8192]{1,0:T(8,128)(2,1)S(1)} %get-tuple-element.7), channel_id=1, source_target_pairs={{0,1},{1,2},{2,3},{3,0},{4,5},{5,6},{6,7},{7,4},{8,9},{9,10},{10,1... | collective-permute-start | bytes 1572872 | tf_op jit(solution)/shard_map/ppermute | solution.py:15
  403.0 14.9 %collective-permute-start.4 = (bf16[32,8192]{1,0:T(8,128)(2,1)S(1)}, bf16[32,8192]{1,0:T(8,128)(2,1)S(1)}, u32[]{:S(2)}, u32[]{:S(2)}) collective-permute-start(bf16[32,8192]{1,0:T(8,128)(2,1)S(1)} %get-tuple-element.7), channel_id=1, source_target_pairs={{0,3},{1,0},{2,1},{3,2},{4,7},{5,4},{6,5},{7,6},{8,11},{9,8},{10,9... | collective-permute-start | bytes 1572872 | tf_op jit(solution)/shard_map/ppermute | solution.py:18
  414.6 8.6 %collective-permute-start.5 = (bf16[32,8192]{1,0:T(8,128)(2,1)S(1)}, bf16[32,8192]{1,0:T(8,128)(2,1)S(1)}, u32[]{:S(2)}, u32[]{:S(2)}) collective-permute-start(bf16[32,8192]{1,0:T(8,128)(2,1)S(1)} %collective-permute-done.3), channel_id=1, source_target_pairs={{0,1},{1,2},{2,3},{3,0},{4,5},{5,6},{6,7},{7,4},{8,9},{9,10},{10,1... | collective-permute-start | bytes 1572872 | tf_op jit(solution)/shard_map/ppermute | solution.py:15
  451.7 142.9 %reduce-scatter.8.cloned.1.call-start = ((), (), s32[]{:S(2)}) async-start(), calls=%async_computation.7 | async-start | bytes 5242880 | tf_op jit(solution)/shard_map/reduce_scatter | solution.py:67
  636.4 51.3 %copy-start.2 = (f32[32,8192]{1,0:T(8,128)}, f32[32,8192]{1,0:T(8,128)S(1)}, u32[]{:S(2)}) copy-start(f32[32,8192]{1,0:T(8,128)S(1)} %multiply_add_fusion) | copy-start | bytes 3145732
Sparse Core Ops, SparseCore 0:
  83.4 41.7 reduce-scatter.3
  176.2 70.1 all-reduce.4
  273.0 43.5 reduce-scatter.5
  451.8 72.6 all-reduce.6
  551.1 43.5 reduce-scatter.7
